TPU v7x, 256 devices: a whole 4x4x8 slice. The times are simulated.
256 devices in a mesh: start: 2 (over core), pencil: 128 (over z, x, y).
Axes of the slice: x: 4, y: 4, z: 8, core: 2. Of those that a mesh axis runs over, the one named last changes fastest.
Arguments:
- template: bfloat16 [512, 64, 512], P('pencil', 'start'), parts along dimension 1, may hold values from -3.5 to 3.5
- reference_image: bfloat16 [512, 64, 512], P('pencil', 'start'), parts along dimension 1, may hold values from -3.5 to 3.5
- velocity: float32 [6, 512, 32, 512], P('start', 'pencil'), parts along dimension 0, may hold values from -4 to 4
- dep_owner: int32 [4, 32768], P('start', 'pencil'), parts along dimension 0, may hold values from 0 to 127, as said below
- dep_offset: int32 [4, 32768], P('start', 'pencil'), parts along dimension 0, may hold values from 0 to 255
- dep_weight: int32 [4, 32768], P('start', 'pencil'), parts along dimension 0, may hold values from 0 to 15
Outputs:
- warped: bfloat16 [512, 64, 512], P('pencil', 'start'), parts along dimension 1
- gradient: float32 [6, 512, 32, 512], P('start', 'pencil'), parts along dimension 0
There are 2 independent parts, one for each index of `start`. A program takes and returns all parts, laid end to end along the dimension named above; each array names one. Nothing has to cross between parts.
Inputs may be any that keep to these rules, and one draw needn't show every extreme that they name: Device d holds blocks d * 256 to (d + 1) * 256 - 1. For a block of device d, dep_owner is (d + m) mod 128 with m one of -2, -1, 0, 1, so that its stencil rows lie on devices d - 2 to d + 2 (modulo 128).
All inputs are finite; a program needn't handle non-finite values.
Results may differ from a plain program's by a relative error of at most 0.012.
Values may be sent and summed in bfloat16 or wider, within the bound.
No kernel may reach another device: no remote copies, remote signals or barrier semaphores. Data moves between devices by JAX's collectives and lax.ppermute only.
A program may use at most 192 MiB of HBM per device.

v0:
```python
import math
import jax
import jax.numpy as jnp
from jax import lax
from jax.sharding import PartitionSpec as P

ZB = 2
SEG = 128
Q = 16
h1_weight = 64.0
force_gain = 32.0


def shifted(x, axis, by):
    length = lax.axis_size(axis)
    return lax.ppermute(x, axis, [(i, (i + by) % length) for i in range(length)])


def dft_tables(length):
    series = jnp.arange(length, dtype=jnp.int32)
    product = series[:, None] * series[None, :] % length
    angles = product.astype(jnp.float32) * (2.0 * math.pi / length)
    return (jnp.cos(angles).astype(jnp.bfloat16), jnp.sin(angles).astype(jnp.bfloat16))


def signed_waves(series, length):
    signed = jnp.where(series < length // 2, series, series - length)
    signed = jnp.where(series == length // 2, 0, signed)
    return signed.astype(jnp.float32) * (2.0 * math.pi / length)


def wave_numbers(length):
    return signed_waves(jnp.arange(length, dtype=jnp.int32), length)


def cubic_table(levels):
    fraction = (jnp.arange(levels, dtype=jnp.float32) + 0.5) / levels
    node_left = -fraction * (fraction - 1.0) * (fraction - 2.0) / 6.0
    node_zero = (fraction + 1.0) * (fraction - 1.0) * (fraction - 2.0) / 2.0
    node_one = -(fraction + 1.0) * fraction * (fraction - 2.0) / 2.0
    node_two = (fraction + 1.0) * fraction * (fraction - 1.0) / 6.0
    return jnp.stack([node_left, node_zero, node_one, node_two], axis=1)


def pick_weights(weight_level, weight_table):
    onehot = (
        weight_level[:, None] == jnp.arange(weight_table.shape[0], dtype=jnp.int32)[None, :]
    ).astype(jnp.float32)
    return jnp.dot(onehot, weight_table, precision=lax.Precision.HIGHEST)


def local(template, reference_image, velocity, dep_owner, dep_offset, dep_weight):
    peer_count = lax.axis_size("pencil")
    row_count, plane_count, y_count = template.shape
    full_rows = row_count * peer_count
    z_groups = plane_count // ZB
    y_groups = y_count // SEG
    per_row = z_groups * y_groups
    block_count = row_count * per_row
    cell_count = plane_count * y_count
    weight_table = cubic_table(Q)
    my_index = lax.axis_index("pencil")
    shaped = template.reshape(row_count, z_groups, ZB, y_groups, SEG)
    blocks = shaped.transpose(0, 1, 3, 2, 4).reshape(block_count, ZB * SEG)
    for section_index in range(2):
        pieces = []
        for distance in (2, 1, 0, -1, -2):
            if distance == 0:
                pieces.append(blocks)
            else:
                pieces.append(shifted(blocks, "pencil", distance))
        window = jnp.concatenate(pieces, axis=0)
        relative = (dep_owner[section_index] - my_index + peer_count) % peer_count
        move = jnp.where(relative >= peer_count - 2, relative - peer_count, relative)
        offset = dep_offset[section_index]
        start_row = offset // per_row
        place = offset % per_row
        tap_row = (
            (move[:, None] + 2) * row_count
            + start_row[:, None]
            + jnp.arange(4, dtype=jnp.int32)[None, :]
        )
        taps = window[tap_row * per_row + place[:, None]].astype(jnp.float32)
        weights = pick_weights(dep_weight[section_index], weight_table)
        blocks = jnp.sum(weights[:, :, None] * taps, axis=1).astype(jnp.bfloat16)
    shaped = blocks.reshape(row_count, z_groups, y_groups, ZB, SEG)
    warped = shaped.transpose(0, 1, 3, 2, 4).reshape(row_count, plane_count, y_count)
    warped_f = warped.astype(jnp.float32)
    residual = reference_image.astype(jnp.float32) - warped_f
    cos_y, sin_y = dft_tables(y_count)
    cos_x, sin_x = dft_tables(full_rows)
    kvec_y = wave_numbers(y_count)
    kvec_x = wave_numbers(full_rows)
    forward_y = jnp.concatenate([cos_y, -sin_y], axis=1)
    inverse_y = jnp.concatenate([cos_y, -sin_y], axis=0)
    forward_x = jnp.concatenate([cos_x, -sin_x], axis=0)
    inverse_x = jnp.concatenate([cos_x, -sin_x], axis=1)
    spec_y = jnp.dot(warped.reshape(-1, y_count), forward_y, preferred_element_type=jnp.float32)
    spec_y = spec_y.astype(jnp.bfloat16).astype(jnp.float32)
    coef_y = jnp.concatenate(
        [-kvec_y * spec_y[:, y_count:], kvec_y * spec_y[:, :y_count]], axis=1
    ).astype(jnp.bfloat16)
    slope_y = (jnp.dot(coef_y, inverse_y, preferred_element_type=jnp.float32) / y_count).reshape(
        row_count, plane_count, y_count
    )
    flat_warp = warped.reshape(1, row_count, cell_count)
    spec_x = jnp.einsum(
        "kx,ixm->ikm",
        forward_x,
        lax.all_to_all(flat_warp, "pencil", split_axis=2, concat_axis=1, tiled=True),
        preferred_element_type=jnp.float32,
    )
    coef_x = jnp.concatenate(
        [
            -kvec_x[None, :, None] * spec_x[:, full_rows:],
            kvec_x[None, :, None] * spec_x[:, :full_rows],
        ],
        axis=1,
    ).astype(jnp.bfloat16)
    slope = (
        jnp.einsum("xk,ikm->ixm", inverse_x, coef_x, preferred_element_type=jnp.float32) / full_rows
    ).astype(jnp.bfloat16)
    slope_x = lax.all_to_all(slope, "pencil", split_axis=1, concat_axis=2, tiled=True)
    slope_x = slope_x.reshape(row_count, plane_count, y_count)
    slope_z = (jnp.roll(warped_f, -1, axis=1) - jnp.roll(warped_f, 1, axis=1)) * 0.5
    force = (jnp.stack([slope_x.astype(jnp.float32), slope_y, slope_z]) * residual[None]).astype(
        jnp.bfloat16
    )
    force_lines = force.reshape(-1, y_count)
    spec_real = jnp.dot(force_lines, cos_y, preferred_element_type=jnp.float32).astype(jnp.bfloat16)
    spec_imag = jnp.dot(force_lines, -sin_y, preferred_element_type=jnp.float32).astype(
        jnp.bfloat16
    )
    spec_f = jnp.stack(
        [spec_real.reshape(3, row_count, cell_count), spec_imag.reshape(3, row_count, cell_count)],
        axis=1,
    )
    planes = lax.all_to_all(spec_f, "pencil", split_axis=3, concat_axis=2, tiled=True)
    local_cols = planes.shape[3]
    column_ids = my_index * local_cols + jnp.arange(local_cols, dtype=jnp.int32)
    kvec_local = signed_waves(column_ids % y_count, y_count)
    spectral_gain = force_gain / (
        full_rows
        * y_count
        * (
            1.0
            + h1_weight
            * (kvec_x[:, None] * kvec_x[:, None] + kvec_local[None, :] * kvec_local[None, :])
        )
    )
    cos_part = jnp.einsum("kx,chxm->chkm", cos_x, planes, preferred_element_type=jnp.float32)
    sin_part = jnp.einsum("kx,chxm->chkm", sin_x, planes, preferred_element_type=jnp.float32)
    real_f = cos_part[:, 0] + sin_part[:, 1]
    imag_f = cos_part[:, 1] - sin_part[:, 0]
    scale_grid = spectral_gain[None]
    scaled = jnp.stack([real_f * scale_grid, imag_f * scale_grid], axis=1).astype(jnp.bfloat16)
    cos_back = jnp.einsum("xk,chkm->chxm", cos_x, scaled, preferred_element_type=jnp.float32)
    sin_back = jnp.einsum("xk,chkm->chxm", sin_x, scaled, preferred_element_type=jnp.float32)
    real_b = cos_back[:, 0] - sin_back[:, 1]
    imag_b = cos_back[:, 1] + sin_back[:, 0]
    mixed = jnp.stack([real_b, imag_b], axis=1).astype(jnp.bfloat16)
    smoothed = lax.all_to_all(mixed, "pencil", split_axis=2, concat_axis=3, tiled=True)
    spatial = jnp.dot(
        smoothed[:, 0].reshape(-1, y_count), cos_y, preferred_element_type=jnp.float32
    )
    spatial = spatial - jnp.dot(
        smoothed[:, 1].reshape(-1, y_count), sin_y, preferred_element_type=jnp.float32
    )
    gradient = velocity + spatial.reshape(3, row_count, plane_count, y_count)
    return (warped, gradient)


def solution(mesh):
    in_specs = (
        P("pencil", "start", None),
        P("pencil", "start", None),
        P("start", "pencil", None, None),
        P("start", "pencil"),
        P("start", "pencil"),
        P("start", "pencil"),
    )
    out_specs = (P("pencil", "start", None), P("start", "pencil", None, None))
    return jax.shard_map(local, mesh=mesh, in_specs=in_specs, out_specs=out_specs, check_vma=False)
```

profile of v0, /device:TPU:2, one launch (start us, length us, event | category | flops | bytes accessed | tf_op | source)
XLA Modules:
  0.0 645.6 jit_solution(7379281555663057057)
XLA Ops:
  0.6 0.9 reshape.587
  1.7 3.3 collective-permute-start
  5.0 0.7 collective-permute-start.1
  5.7 3.5 collective-permute-start.2
  9.2 0.8 fusion.101
  9.9 0.8 subtract_add_fusion
  11.0 0.8 fusion.100
  12.5 3.9 cosine_convert_fusion
  16.6 3.9 gather_fusion
  20.8 0.7 multiply_reduce_fusion.1
  21.6 3.6 collective-permute-start.4
  25.2 4.0 fusion.20
  29.3 4.1 collective-permute-start.6
  33.4 1.7 collective-permute-start.7
  35.1 1.8 collective-permute-done.5
  36.9 3.4 collective-permute-done.7
  40.3 3.9 gather_fusion.1
  44.5 0.7 multiply_reduce_fusion
  45.5 12.9 %copy.100 = bf16[1,4,16384]{1,0,2:T(2,128)(2,1)} copy(bf16[1,4,16384]{2,1,0:T(4,128)(2,1)S(1)} %reshape_reshape.6) | data formatting | bytes 262144 | tf_op jit(solution)/shard_map/reshape;reshape | solution.py:106
  58.9 90.7 %reduce = bf16[16384,4]{1,0:T(8,128)(2,1)} reduce(bf16[16384,1,4]{2,1,0:T(2,128)(2,1)} %bitcast.108, bf16[]{:T(256)} %broadcast.922), dimensions={1}, to_apply=%bitcast.90.reduce_sub_computation | reduce | bytes 262146
  149.6 9.3 %reshape.616 = bf16[128,2,256]{2,1,0:T(2,128)(2,1)} reshape(bf16[16384,4]{1,0:T(8,128)(2,1)} %reduce) | data formatting | bytes 262144
  158.9 19.8 %all-to-all-start = ((bf16[128,2,256]{2,1,0:T(2,128)(2,1)}), bf16[128,2,256]{2,1,0:T(2,128)(2,1)S(1)}, u32[]{:S(2)}, u32[]{:S(2)}) async-start(bf16[128,2,256]{2,1,0:T(2,128)(2,1)} %reshape.616), calls=%async_computation | async-start | bytes 262144 | tf_op jit(solution)/shard_map/all_to_all | solution.py:110
  179.5 11.0 %all-to-all-done = bf16[128,2,256]{2,1,0:T(2,128)(2,1)S(1)} async-done(((bf16[128,2,256]{2,1,0:T(2,128)(2,1)}), bf16[128,2,256]{2,1,0:T(2,128)(2,1)S(1)}, u32[]{:S(2)}, u32[]{:S(2)}) %all-to-all-start) | async-done | bytes 131104 | tf_op jit(solution)/shard_map/all_to_all | solution.py:110
  190.4 17.1 %reshape.617 = bf16[16384,1,4]{2,1,0:T(2,128)(2,1)} reshape(bf16[128,2,256]{2,1,0:T(2,128)(2,1)S(1)} %all-to-all-done) | data formatting | bytes 262144
  207.5 15.4 %copy.101 = bf16[1,4,16384]{2,1,0:T(4,128)(2,1)S(1)} copy(bf16[1,4,16384]{1,0,2:T(2,128)(2,1)} %bitcast.109) | data formatting | bytes 262144 | tf_op jit(solution)/shard_map/all_to_all | solution.py:110
  224.3 1.3 reduce.1
  225.6 0.7 reshape.618
  226.4 6.6 %all-to-all-start.1 = ((bf16[128,2,256]{2,1,0:T(2,128)(2,1)}), bf16[128,2,256]{2,1,0:T(2,128)(2,1)S(1)}, u32[]{:S(2)}, u32[]{:S(2)}) async-start(bf16[128,2,256]{2,1,0:T(2,128)(2,1)} %reshape.618), calls=%async_computation.1 | async-start | bytes 262144 | tf_op jit(solution)/shard_map/all_to_all | solution.py:123
  233.1 11.8 %all-to-all-done.1 = bf16[128,2,256]{2,1,0:T(2,128)(2,1)S(1)} async-done(((bf16[128,2,256]{2,1,0:T(2,128)(2,1)}), bf16[128,2,256]{2,1,0:T(2,128)(2,1)S(1)}, u32[]{:S(2)}, u32[]{:S(2)}) %all-to-all-start.1) | async-done | bytes 131104 | tf_op jit(solution)/shard_map/all_to_all | solution.py:123
  245.3 4.8 convolution_convert_fusion.1
  250.1 4.9 convolution_convert_fusion
  255.3 39.4 %copy.107 = bf16[3,1,4,16384]{2,1,0,3:T(2,128)(2,1)} copy(bf16[3,1,4,16384]{3,2,0,1:T(4,128)(2,1)S(1)} %stack_reshape.10) | data formatting | bytes 786432 | tf_op jit(solution)/shard_map/stack;reshape | solution.py:134
  294.9 39.6 %copy.108 = bf16[3,1,4,16384]{2,1,0,3:T(2,128)(2,1)} copy(bf16[3,1,4,16384]{3,2,0,1:T(4,128)(2,1)S(1)} %stack_reshape.11) | data formatting | bytes 786432 | tf_op jit(solution)/shard_map/stack;reshape | solution.py:134
  334.5 70.4 %fusion.102 = bf16[16384,3,2,4]{3,2,1,0:T(2,128)(2,1)} fusion(bf16[3,1,4,16384]{2,1,0,3:T(2,128)(2,1)} %copy.108, bf16[3,1,4,16384]{2,1,0,3:T(2,128)(2,1)} %copy.107), kind=kLoop, calls=%fused_computation.201 | loop fusion | flops 1572864 | bytes 1572864
  404.9 61.9 %reshape.620 = bf16[128,2,1536]{2,1,0:T(2,128)(2,1)} reshape(bf16[16384,3,2,4]{3,2,1,0:T(2,128)(2,1)} %fusion.102) | data formatting | bytes 1572864
  466.8 7.0 %all-to-all-start.2 = ((bf16[128,2,1536]{2,1,0:T(2,128)(2,1)}), bf16[128,2,1536]{2,1,0:T(2,128)(2,1)S(1)}, u32[]{:S(2)}, u32[]{:S(2)}) async-start(bf16[128,2,1536]{2,1,0:T(2,128)(2,1)} %reshape.620), calls=%async_computation.2 | async-start | bytes 1572864 | tf_op jit(solution)/shard_map/all_to_all | solution.py:138
  474.0 20.2 %all-to-all-done.2 = bf16[128,2,1536]{2,1,0:T(2,128)(2,1)S(1)} async-done(((bf16[128,2,1536]{2,1,0:T(2,128)(2,1)}), bf16[128,2,1536]{2,1,0:T(2,128)(2,1)S(1)}, u32[]{:S(2)}, u32[]{:S(2)}) %all-to-all-start.2) | async-done | bytes 786464 | tf_op jit(solution)/shard_map/all_to_all | solution.py:138
  494.2 55.1 %reshape.621 = bf16[16384,3,2,4]{3,2,1,0:T(2,128)(2,1)} reshape(bf16[128,2,1536]{2,1,0:T(2,128)(2,1)S(1)} %all-to-all-done.2) | data formatting | bytes 1572864
  549.3 35.1 %copy.121 = bf16[3,2,4,128,128]{4,3,2,1,0:T(8,128)(2,1)S(1)} copy(bf16[3,2,4,128,128]{2,1,0,4,3:T(2,128)(2,1)} %bitcast.107) | data formatting | bytes 1572864 | tf_op jit(solution)/shard_map/all_to_all | solution.py:138
  585.0 5.5 convolution_bitcast_fusion.2
  590.5 5.9 convolution_bitcast_fusion.3
  596.9 4.3 convolution_bitcast_fusion.1
  601.1 4.3 convolution_bitcast_fusion
  605.9 1.1 copy.113
  607.1 27.0 %all_to_all.60 = bf16[3,2,512,128]{3,1,0,2:T(2,128)(2,1)S(1)} all-to-all(bf16[3,2,512,128]{3,1,0,2:T(2,128)(2,1)S(1)} %copy.113), channel_id=1, replica_groups=mesh['start'=2,'pencil'=128] {'pencil'}, dimensions={2} | all-to-all | bytes 1572864 | tf_op jit(solution)/shard_map/all_to_all | solution.py:162
  634.8 4.6 fusion.21
  639.7 4.7 convolution_subtract_fusion
  644.4 1.0 add.429
  (79 shorter events, 8.3 us)
Async XLA Ops:
  1.7 14.8 %collective-permute-start = (bf16[256,256]{1,0:T(8,128)(2,1)S(1)}, bf16[256,256]{1,0:T(8,128)(2,1)S(1)}, u32[]{:S(2)}, u32[]{:S(2)}) collective-permute-start(bf16[256,256]{1,0:T(8,128)(2,1)S(1)} %bitcast.127), channel_id=1, source_target_pairs={{0,2},{1,3},{2,4},{3,5},{4,6},{5,7},{6,8},{7,9},{8,10},{9,11},{10,... | collective-permute-start | bytes 393224 | tf_op jit(solution)/shard_map/ppermute | solution.py:16
  5.0 11.5 %collective-permute-start.1 = (bf16[256,256]{1,0:T(8,128)(2,1)S(1)}, bf16[256,256]{1,0:T(8,128)(2,1)S(1)}, u32[]{:S(2)}, u32[]{:S(2)}) collective-permute-start(bf16[256,256]{1,0:T(8,128)(2,1)S(1)} %bitcast.128), channel_id=1, source_target_pairs={{0,1},{1,2},{2,3},{3,4},{4,5},{5,6},{6,7},{7,8},{8,9},{9,10},{10,1... | collective-permute-start | bytes 393224 | tf_op jit(solution)/shard_map/ppermute | solution.py:16
  5.7 10.9 %collective-permute-start.2 = (bf16[256,256]{1,0:T(8,128)(2,1)S(1)}, bf16[256,256]{1,0:T(8,128)(2,1)S(1)}, u32[]{:S(2)}, u32[]{:S(2)}) collective-permute-start(bf16[256,256]{1,0:T(8,128)(2,1)S(1)} %bitcast.129), channel_id=1, source_target_pairs={{0,127},{1,0},{2,1},{3,2},{4,3},{5,4},{6,5},{7,6},{8,7},{9,8},{10,... | collective-permute-start | bytes 393224 | tf_op jit(solution)/shard_map/ppermute | solution.py:16
  9.1 7.5 %collective-permute-start.3 = (bf16[256,256]{1,0:T(8,128)(2,1)S(1)}, bf16[256,256]{1,0:T(8,128)(2,1)S(1)}, u32[]{:S(2)}, u32[]{:S(2)}) collective-permute-start(bf16[256,256]{1,0:T(8,128)(2,1)S(1)} %bitcast.130), channel_id=1, source_target_pairs={{0,126},{1,127},{2,0},{3,1},{4,2},{5,3},{6,4},{7,5},{8,6},{9,7},{1... | collective-permute-start | bytes 393224 | tf_op jit(solution)/shard_map/ppermute | solution.py:16
  21.6 13.5 %collective-permute-start.4 = (bf16[256,256]{1,0:T(8,128)(2,1)S(1)}, bf16[256,256]{1,0:T(8,128)(2,1)S(1)}, u32[]{:S(2)}, u32[]{:S(2)}) collective-permute-start(bf16[256,256]{1,0:T(8,128)(2,1)S(1)} %multiply_reduce_fusion.1), channel_id=1, source_target_pairs={{0,2},{1,3},{2,4},{3,5},{4,6},{5,7},{6,8},{7,9},{8,10},{9,11},{10,... | collective-permute-start | bytes 393224 | tf_op jit(solution)/shard_map/ppermute | solution.py:16
  29.2 7.7 %collective-permute-start.5 = (bf16[256,256]{1,0:T(8,128)(2,1)S(1)}, bf16[256,256]{1,0:T(8,128)(2,1)S(1)}, u32[]{:S(2)}, u32[]{:S(2)}) collective-permute-start(bf16[256,256]{1,0:T(8,128)(2,1)S(1)} %multiply_reduce_fusion.1), channel_id=1, source_target_pairs={{0,1},{1,2},{2,3},{3,4},{4,5},{5,6},{6,7},{7,8},{8,9},{9,10},{10,1... | collective-permute-start | bytes 393224 | tf_op jit(solution)/shard_map/ppermute | solution.py:16
  29.3 7.6 %collective-permute-start.6 = (bf16[256,256]{1,0:T(8,128)(2,1)S(1)}, bf16[256,256]{1,0:T(8,128)(2,1)S(1)}, u32[]{:S(2)}, u32[]{:S(2)}) collective-permute-start(bf16[256,256]{1,0:T(8,128)(2,1)S(1)} %multiply_reduce_fusion.1), channel_id=1, source_target_pairs={{0,127},{1,0},{2,1},{3,2},{4,3},{5,4},{6,5},{7,6},{8,7},{9,8},{10,... | collective-permute-start | bytes 393224 | tf_op jit(solution)/shard_map/ppermute | solution.py:16
  33.4 6.9 %collective-permute-start.7 = (bf16[256,256]{1,0:T(8,128)(2,1)S(1)}, bf16[256,256]{1,0:T(8,128)(2,1)S(1)}, u32[]{:S(2)}, u32[]{:S(2)}) collective-permute-start(bf16[256,256]{1,0:T(8,128)(2,1)S(1)} %multiply_reduce_fusion.1), channel_id=1, source_target_pairs={{0,126},{1,127},{2,0},{3,1},{4,2},{5,3},{6,4},{7,5},{8,6},{9,7},{1... | collective-permute-start | bytes 393224 | tf_op jit(solution)/shard_map/ppermute | solution.py:16
  45.5 187.6 %copy-start = (bf16[4,32,512]{2,1,0:T(8,128)(2,1)}, bf16[4,32,512]{2,1,0:T(8,128)(2,1)S(1)}, u32[]{:S(2)}) copy-start(bf16[4,32,512]{2,1,0:T(8,128)(2,1)S(1)} %reshape.589) | copy-start | bytes 393220
  158.9 31.5 %all-to-all-start = ((bf16[128,2,256]{2,1,0:T(2,128)(2,1)}), bf16[128,2,256]{2,1,0:T(2,128)(2,1)S(1)}, u32[]{:S(2)}, u32[]{:S(2)}) async-start(bf16[128,2,256]{2,1,0:T(2,128)(2,1)} %reshape.616), calls=%async_computation | async-start | bytes 262144 | tf_op jit(solution)/shard_map/all_to_all | solution.py:110
  223.6 9.4 %copy-start.2 = (bf16[4,32,512]{2,1,0:T(8,128)(2,1)S(1)}, bf16[4,32,512]{2,1,0:T(8,128)(2,1)}, u32[]{:S(2)}) copy-start(bf16[4,32,512]{2,1,0:T(8,128)(2,1)} %param.7) | copy-start | bytes 393220
  226.4 18.5 %all-to-all-start.1 = ((bf16[128,2,256]{2,1,0:T(2,128)(2,1)}), bf16[128,2,256]{2,1,0:T(2,128)(2,1)S(1)}, u32[]{:S(2)}, u32[]{:S(2)}) async-start(bf16[128,2,256]{2,1,0:T(2,128)(2,1)} %reshape.618), calls=%async_computation.1 | async-start | bytes 262144 | tf_op jit(solution)/shard_map/all_to_all | solution.py:123
  466.8 27.4 %all-to-all-start.2 = ((bf16[128,2,1536]{2,1,0:T(2,128)(2,1)}), bf16[128,2,1536]{2,1,0:T(2,128)(2,1)S(1)}, u32[]{:S(2)}, u32[]{:S(2)}) async-start(bf16[128,2,1536]{2,1,0:T(2,128)(2,1)} %reshape.620), calls=%async_computation.2 | async-start | bytes 1572864 | tf_op jit(solution)/shard_map/all_to_all | solution.py:138
  639.7 4.7 copy-start.1
where the time goes:
time: 654 us; the launch traced here: 646 us
  local copies, waits for them, and re-layouts  302 us (46%)
  other arithmetic  175 us (27%)
  starting transfers between devices  50.2 us (8%)
  waiting for transfers between devices  48.2 us (7%)
  matrix products  41.1 us (6%)
  blocking collectives  27 us (4%)
    unnamed x3, other arithmetic  162 us
    unnamed x23, local copies, waits for them, and re-layouts  145 us
    another operation x4, local copies, waits for them, and re-layouts, local(): jnp.stack([spec_real.reshape(3, row_count, cell_count), spec_imag.reshape...  79.5 us
    all_to_all x2, local copies, waits for them, and re-layouts, local(): lax.all_to_all(spec_f, 'pencil', split_axis=3, concat_axis=2, tiled=True)  35.7 us
    all_to_all x1, blocking collectives, local(): lax.all_to_all(mixed, 'pencil', split_axis=2, concat_axis=3, tiled=True)  27 us
    all_to_all x1, waiting for transfers between devices, local(): lax.all_to_all(spec_f, 'pencil', split_axis=3, concat_axis=2, tiled=True)  20.2 us
    all_to_all x1, starting transfers between devices, local(): lax.all_to_all(flat_warp, 'pencil', split_axis=2, concat_axis=1, tiled=True)  19.8 us
    ppermute x8, starting transfers between devices, shifted(): lax.ppermute(x, axis, [(i, (i + by) % length) for i in range(length)])  16.9 us
  transfers between devices with their start and end apart: 11, of which 5 were waited for; matrix products, arithmetic and copies ran while one was open for 2% of the time, Pallas kernels for 0%

commit v1 on v0

--- a/solution.py
+++ b/solution.py
@@ -135,7 +135,10 @@
         [spec_real.reshape(3, row_count, cell_count), spec_imag.reshape(3, row_count, cell_count)],
         axis=1,
     )
-    planes = lax.all_to_all(spec_f, "pencil", split_axis=3, concat_axis=2, tiled=True)
+    devices = lax.axis_size("pencil")
+    shards = jnp.stack(jnp.split(spec_f, devices, axis=3), axis=0)
+    shards = lax.all_to_all(shards, "pencil", split_axis=0, concat_axis=0)
+    planes = jnp.concatenate(shards, axis=2)
     local_cols = planes.shape[3]
     column_ids = my_index * local_cols + jnp.arange(local_cols, dtype=jnp.int32)
     kvec_local = signed_waves(column_ids % y_count, y_count)

time: 654 us -> 440 us (0.67)
  local copies, waits for them, and re-layouts: 302 us -> 70.9 us
  starting transfers between devices: 50.2 us -> 61.3 us
  other arithmetic: 175 us -> 182 us
    unnamed x23 -> x21, local copies, waits for them, and re-layouts: 145 us -> 27.9 us
    another operation x4 -> x2, local copies, waits for them, and re-layouts: 79.5 us -> 0.57 us  [local(): jnp.stack([spec_real.reshape(3, row_count, cell_count), spec_imag.reshape...]
    all_to_all x2 -> x0, local copies, waits for them, and re-layouts: 35.7 us -> none  [local(): lax.all_to_all(spec_f, 'pencil', split_axis=3, concat_axis=2, tiled=True)]
    all_to_all x1, starting transfers between devices: 19.8 us -> 31.4 us  [local(): lax.all_to_all(flat_warp, 'pencil', split_axis=2, concat_axis=1, tiled=True)]
    unnamed x3 -> x129, other arithmetic: 162 us -> 168 us
  transfers between devices with their start and end apart: 11 -> 11, of which waited for: 5 -> 5; matrix products, arithmetic and copies ran while one was open for 2% -> 3% of each run, Pallas kernels for 0% -> 0%
where the time goes in v1:
time: 440 us; the launch traced here: 432 us
  other arithmetic  182 us (41%)
  local copies, waits for them, and re-layouts  70.9 us (16%)
  starting transfers between devices  61.3 us (14%)
  waiting for transfers between devices  48.3 us (11%)
  matrix products  40.9 us (9%)
  blocking collectives  27.1 us (6%)
    unnamed x129, other arithmetic  168 us
    all_to_all x1, starting transfers between devices, local(): lax.all_to_all(flat_warp, 'pencil', split_axis=2, concat_axis=1, tiled=True)  31.4 us
    unnamed x21, local copies, waits for them, and re-layouts  27.9 us
    all_to_all x1, blocking collectives, local(): lax.all_to_all(mixed, 'pencil', split_axis=2, concat_axis=3, tiled=True)  27.1 us
    all_to_all x1, waiting for transfers between devices, local(): shards = lax.all_to_all(shards, 'pencil', split_axis=0, concat_axis=0)  20.3 us
    ppermute x8, starting transfers between devices, shifted(): lax.ppermute(x, axis, [(i, (i + by) % length) for i in range(length)])  16.7 us
    all_to_all x2, local copies, waits for them, and re-layouts, local(): lax.all_to_all(flat_warp, 'pencil', split_axis=2, concat_axis=1, tiled=True)  15.5 us
    another operation x2, local copies, waits for them, and re-layouts, local(): flat_warp = warped.reshape(1, row_count, cell_count)  13 us
  transfers between devices with their start and end apart: 11, of which 5 were waited for; matrix products, arithmetic and copies ran while one was open for 3% of the time, Pallas kernels for 0%

profile of v1, /device:TPU:2, one launch (start us, length us, event | category | flops | bytes accessed | tf_op | source)
XLA Modules:
  0.0 431.9 jit_solution(3721829388552712221)
XLA Ops:
  0.6 0.9 reshape.593
  1.7 3.3 collective-permute-start
  5.0 0.7 collective-permute-start.1
  5.7 3.5 collective-permute-start.2
  9.2 0.8 fusion.229
  9.9 0.8 subtract_add_fusion
  11.0 0.8 fusion.228
  12.5 3.9 cosine_convert_fusion
  16.6 3.9 gather_fusion
  20.8 0.7 multiply_reduce_fusion.1
  21.6 3.6 collective-permute-start.4
  25.2 4.0 fusion.20
  29.3 4.1 collective-permute-start.6
  33.4 1.5 collective-permute-start.7
  34.9 2.2 collective-permute-done.5
  37.1 3.0 collective-permute-done.7
  40.1 3.9 gather_fusion.1
  44.3 0.7 multiply_reduce_fusion
  45.3 12.9 %copy.313 = bf16[1,4,16384]{1,0,2:T(2,128)(2,1)} copy(bf16[1,4,16384]{2,1,0:T(4,128)(2,1)S(1)} %reshape_reshape.6) | data formatting | bytes 262144 | tf_op jit(solution)/shard_map/reshape;reshape | solution.py:106
  58.7 90.7 %reduce = bf16[16384,4]{1,0:T(8,128)(2,1)} reduce(bf16[16384,1,4]{2,1,0:T(2,128)(2,1)} %bitcast.619, bf16[]{:T(256)} %broadcast.922), dimensions={1}, to_apply=%bitcast.349.reduce_sub_computation | reduce | bytes 262146
  149.4 9.3 %reshape.624 = bf16[128,2,256]{2,1,0:T(2,128)(2,1)} reshape(bf16[16384,4]{1,0:T(8,128)(2,1)} %reduce) | data formatting | bytes 262144
  158.7 31.4 %all-to-all-start = ((bf16[128,2,256]{2,1,0:T(2,128)(2,1)}), bf16[128,2,256]{2,1,0:T(2,128)(2,1)S(1)}, u32[]{:S(2)}, u32[]{:S(2)}) async-start(bf16[128,2,256]{2,1,0:T(2,128)(2,1)} %reshape.624), calls=%async_computation | async-start | bytes 262144 | tf_op jit(solution)/shard_map/all_to_all | solution.py:110
  190.8 11.0 %all-to-all-done = bf16[128,2,256]{2,1,0:T(2,128)(2,1)S(1)} async-done(((bf16[128,2,256]{2,1,0:T(2,128)(2,1)}), bf16[128,2,256]{2,1,0:T(2,128)(2,1)S(1)}, u32[]{:S(2)}, u32[]{:S(2)}) %all-to-all-start) | async-done | bytes 131104 | tf_op jit(solution)/shard_map/all_to_all | solution.py:110
  201.8 17.1 %reshape.625 = bf16[16384,1,4]{2,1,0:T(2,128)(2,1)} reshape(bf16[128,2,256]{2,1,0:T(2,128)(2,1)S(1)} %all-to-all-done) | data formatting | bytes 262144
  218.9 15.4 %copy.314 = bf16[1,4,16384]{2,1,0:T(4,128)(2,1)S(1)} copy(bf16[1,4,16384]{1,0,2:T(2,128)(2,1)} %bitcast.620) | data formatting | bytes 262144 | tf_op jit(solution)/shard_map/all_to_all | solution.py:110
  235.6 1.3 reduce.1
  237.0 0.7 reshape.626
  237.7 6.6 %all-to-all-start.1 = ((bf16[128,2,256]{2,1,0:T(2,128)(2,1)}), bf16[128,2,256]{2,1,0:T(2,128)(2,1)S(1)}, u32[]{:S(2)}, u32[]{:S(2)}) async-start(bf16[128,2,256]{2,1,0:T(2,128)(2,1)} %reshape.626), calls=%async_computation.1 | async-start | bytes 262144 | tf_op jit(solution)/shard_map/all_to_all | solution.py:123
  244.5 11.8 %all-to-all-done.1 = bf16[128,2,256]{2,1,0:T(2,128)(2,1)S(1)} async-done(((bf16[128,2,256]{2,1,0:T(2,128)(2,1)}), bf16[128,2,256]{2,1,0:T(2,128)(2,1)S(1)}, u32[]{:S(2)}, u32[]{:S(2)}) %all-to-all-start.1) | async-done | bytes 131104 | tf_op jit(solution)/shard_map/all_to_all | solution.py:123
  256.6 4.8 %convolution_convert_fusion.1 = bf16[384,512]{1,0:T(8,128)(2,1)S(1)} fusion(bf16[384,512]{1,0:T(8,128)(2,1)S(1)} %bitcast.635), kind=kOutput, calls=%fused_computation.265 | convolution fusion | flops 205455360 | bytes 786432 | tf_op jit(solution)/shard_map/dot_general | solution.py:130
  261.5 4.9 %convolution_convert_fusion = bf16[384,512]{1,0:T(8,128)(2,1)S(1)} fusion(bf16[384,512]{1,0:T(8,128)(2,1)S(1)} %bitcast.636), kind=kOutput, calls=%fused_computation.264 | convolution fusion | flops 206241792 | bytes 786432 | tf_op jit(solution)/shard_map/dot_general | solution.py:131
  266.9 0.6 constant_dynamic-update-slice_fusion.137
  267.5 0.6 constant_dynamic-update-slice_fusion.136
  269.3 0.6 constant_dynamic-update-slice_fusion.133
  271.1 0.6 constant_dynamic-update-slice_fusion.130
  272.9 0.6 constant_dynamic-update-slice_fusion.127
  274.7 0.6 constant_dynamic-update-slice_fusion.124
  343.7 6.6 %all-to-all-start.2 = ((bf16[128,3,2,4,128]{4,3,2,1,0:T(4,128)(2,1)}), bf16[128,3,2,4,128]{4,3,2,1,0:T(4,128)(2,1)S(1)}, u32[]{:S(2)}, u32[]{:S(2)}) async-start(bf16[128,3,2,4,128]{4,3,2,1,0:T(4,128)(2,1)} %constant_dynamic-update-slice_fusion.10), calls=%async_computation.2 | async-start | bytes 1572864 | tf_op jit(solution)/shard_map/all_to_all | solution.py:140
  350.5 20.3 %all-to-all-done.2 = bf16[128,3,2,4,128]{4,3,2,1,0:T(4,128)(2,1)S(1)} async-done(((bf16[128,3,2,4,128]{4,3,2,1,0:T(4,128)(2,1)}), bf16[128,3,2,4,128]{4,3,2,1,0:T(4,128)(2,1)S(1)}, u32[]{:S(2)}, u32[]{:S(2)}) %all-to-all-start.2) | async-done | bytes 786464 | tf_op jit(solution)/shard_map/all_to_all | solution.py:140
  371.1 5.6 %convolution_bitcast_fusion.2 = f32[3,2,512,128]{2,3,1,0:T(8,128)S(1)} fusion(bf16[3,2,512,128]{3,2,1,0:T(8,128)(2,1)S(1)} %bitcast.628), kind=kOutput, calls=%fused_computation.261 | convolution fusion | flops 406585344 | bytes 2359296 | tf_op jit(solution)/shard_map/kx,chxm->chkm/dot_general | solution.py:155
  376.6 5.7 %convolution_bitcast_fusion.3 = f32[3,2,512,128]{2,3,1,0:T(8,128)S(1)} fusion(bf16[3,2,512,128]{3,2,1,0:T(8,128)(2,1)S(1)} %bitcast.629), kind=kOutput, calls=%fused_computation.262 | convolution fusion | flops 406585344 | bytes 2359296 | tf_op jit(solution)/shard_map/kx,chxm->chkm/dot_general | solution.py:154
  382.8 4.3 convolution_bitcast_fusion.1
  387.1 4.3 convolution_bitcast_fusion
  391.9 1.1 copy.325
  393.0 27.1 %all_to_all.47 = bf16[3,2,512,128]{3,1,0,2:T(2,128)(2,1)S(1)} all-to-all(bf16[3,2,512,128]{3,1,0,2:T(2,128)(2,1)S(1)} %copy.325), channel_id=1, replica_groups=mesh['start'=2,'pencil'=128] {'pencil'}, dimensions={2} | all-to-all | bytes 1572864 | tf_op jit(solution)/shard_map/all_to_all | solution.py:165
  420.8 4.6 %fusion.21 = f32[384,512]{1,0:T(8,128)S(1)} fusion(bf16[384,512]{1,0:T(8,128)(2,1)S(1)} %reshape_squeeze.6), kind=kOutput, calls=%fused_computation.304 | convolution fusion | flops 205258752 | bytes 1179648 | tf_op jit(solution)/shard_map/dot_general | solution.py:166
  425.7 4.7 %convolution_subtract_fusion = f32[384,512]{1,0:T(8,128)S(1)} fusion(f32[384,512]{1,0:T(8,128)S(1)} %fusion.21, bf16[384,512]{1,0:T(8,128)(2,1)S(1)} %reshape_squeeze.7), kind=kOutput, calls=%fused_computation.263 | convolution fusion | flops 205455360 | bytes 1966080 | tf_op jit(solution)/shard_map/dot_general | solution.py:169
  430.4 1.0 add.429
  (201 shorter events, 81.1 us)
Async XLA Ops:
  1.7 14.8 %collective-permute-start = (bf16[256,256]{1,0:T(8,128)(2,1)S(1)}, bf16[256,256]{1,0:T(8,128)(2,1)S(1)}, u32[]{:S(2)}, u32[]{:S(2)}) collective-permute-start(bf16[256,256]{1,0:T(8,128)(2,1)S(1)} %bitcast.638), channel_id=1, source_target_pairs={{0,2},{1,3},{2,4},{3,5},{4,6},{5,7},{6,8},{7,9},{8,10},{9,11},{10,... | collective-permute-start | bytes 393224 | tf_op jit(solution)/shard_map/ppermute | solution.py:16
  5.0 11.5 %collective-permute-start.1 = (bf16[256,256]{1,0:T(8,128)(2,1)S(1)}, bf16[256,256]{1,0:T(8,128)(2,1)S(1)}, u32[]{:S(2)}, u32[]{:S(2)}) collective-permute-start(bf16[256,256]{1,0:T(8,128)(2,1)S(1)} %bitcast.639), channel_id=1, source_target_pairs={{0,1},{1,2},{2,3},{3,4},{4,5},{5,6},{6,7},{7,8},{8,9},{9,10},{10,1... | collective-permute-start | bytes 393224 | tf_op jit(solution)/shard_map/ppermute | solution.py:16
  5.7 10.9 %collective-permute-start.2 = (bf16[256,256]{1,0:T(8,128)(2,1)S(1)}, bf16[256,256]{1,0:T(8,128)(2,1)S(1)}, u32[]{:S(2)}, u32[]{:S(2)}) collective-permute-start(bf16[256,256]{1,0:T(8,128)(2,1)S(1)} %bitcast.640), channel_id=1, source_target_pairs={{0,127},{1,0},{2,1},{3,2},{4,3},{5,4},{6,5},{7,6},{8,7},{9,8},{10,... | collective-permute-start | bytes 393224 | tf_op jit(solution)/shard_map/ppermute | solution.py:16
  9.1 7.5 %collective-permute-start.3 = (bf16[256,256]{1,0:T(8,128)(2,1)S(1)}, bf16[256,256]{1,0:T(8,128)(2,1)S(1)}, u32[]{:S(2)}, u32[]{:S(2)}) collective-permute-start(bf16[256,256]{1,0:T(8,128)(2,1)S(1)} %bitcast.641), channel_id=1, source_target_pairs={{0,126},{1,127},{2,0},{3,1},{4,2},{5,3},{6,4},{7,5},{8,6},{9,7},{1... | collective-permute-start | bytes 393224 | tf_op jit(solution)/shard_map/ppermute | solution.py:16
  21.6 13.3 %collective-permute-start.4 = (bf16[256,256]{1,0:T(8,128)(2,1)S(1)}, bf16[256,256]{1,0:T(8,128)(2,1)S(1)}, u32[]{:S(2)}, u32[]{:S(2)}) collective-permute-start(bf16[256,256]{1,0:T(8,128)(2,1)S(1)} %multiply_reduce_fusion.1), channel_id=1, source_target_pairs={{0,2},{1,3},{2,4},{3,5},{4,6},{5,7},{6,8},{7,9},{8,10},{9,11},{10,... | collective-permute-start | bytes 393224 | tf_op jit(solution)/shard_map/ppermute | solution.py:16
  29.2 7.9 %collective-permute-start.5 = (bf16[256,256]{1,0:T(8,128)(2,1)S(1)}, bf16[256,256]{1,0:T(8,128)(2,1)S(1)}, u32[]{:S(2)}, u32[]{:S(2)}) collective-permute-start(bf16[256,256]{1,0:T(8,128)(2,1)S(1)} %multiply_reduce_fusion.1), channel_id=1, source_target_pairs={{0,1},{1,2},{2,3},{3,4},{4,5},{5,6},{6,7},{7,8},{8,9},{9,10},{10,1... | collective-permute-start | bytes 393224 | tf_op jit(solution)/shard_map/ppermute | solution.py:16
  29.3 7.8 %collective-permute-start.6 = (bf16[256,256]{1,0:T(8,128)(2,1)S(1)}, bf16[256,256]{1,0:T(8,128)(2,1)S(1)}, u32[]{:S(2)}, u32[]{:S(2)}) collective-permute-start(bf16[256,256]{1,0:T(8,128)(2,1)S(1)} %multiply_reduce_fusion.1), channel_id=1, source_target_pairs={{0,127},{1,0},{2,1},{3,2},{4,3},{5,4},{6,5},{7,6},{8,7},{9,8},{10,... | collective-permute-start | bytes 393224 | tf_op jit(solution)/shard_map/ppermute | solution.py:16
  33.4 6.7 %collective-permute-start.7 = (bf16[256,256]{1,0:T(8,128)(2,1)S(1)}, bf16[256,256]{1,0:T(8,128)(2,1)S(1)}, u32[]{:S(2)}, u32[]{:S(2)}) collective-permute-start(bf16[256,256]{1,0:T(8,128)(2,1)S(1)} %multiply_reduce_fusion.1), channel_id=1, source_target_pairs={{0,126},{1,127},{2,0},{3,1},{4,2},{5,3},{6,4},{7,5},{8,6},{9,7},{1... | collective-permute-start | bytes 393224 | tf_op jit(solution)/shard_map/ppermute | solution.py:16
  45.3 199.2 %copy-start = (bf16[4,32,512]{2,1,0:T(8,128)(2,1)}, bf16[4,32,512]{2,1,0:T(8,128)(2,1)S(1)}, u32[]{:S(2)}) copy-start(bf16[4,32,512]{2,1,0:T(8,128)(2,1)S(1)} %reshape.595) | copy-start | bytes 393220
  158.7 43.1 %all-to-all-start = ((bf16[128,2,256]{2,1,0:T(2,128)(2,1)}), bf16[128,2,256]{2,1,0:T(2,128)(2,1)S(1)}, u32[]{:S(2)}, u32[]{:S(2)}) async-start(bf16[128,2,256]{2,1,0:T(2,128)(2,1)} %reshape.624), calls=%async_computation | async-start | bytes 262144 | tf_op jit(solution)/shard_map/all_to_all | solution.py:110
  235.0 9.5 %copy-start.2 = (bf16[4,32,512]{2,1,0:T(8,128)(2,1)S(1)}, bf16[4,32,512]{2,1,0:T(8,128)(2,1)}, u32[]{:S(2)}) copy-start(bf16[4,32,512]{2,1,0:T(8,128)(2,1)} %param.7) | copy-start | bytes 393220
  237.7 18.5 %all-to-all-start.1 = ((bf16[128,2,256]{2,1,0:T(2,128)(2,1)}), bf16[128,2,256]{2,1,0:T(2,128)(2,1)S(1)}, u32[]{:S(2)}, u32[]{:S(2)}) async-start(bf16[128,2,256]{2,1,0:T(2,128)(2,1)} %reshape.626), calls=%async_computation.1 | async-start | bytes 262144 | tf_op jit(solution)/shard_map/all_to_all | solution.py:123
  343.7 27.1 %all-to-all-start.2 = ((bf16[128,3,2,4,128]{4,3,2,1,0:T(4,128)(2,1)}), bf16[128,3,2,4,128]{4,3,2,1,0:T(4,128)(2,1)S(1)}, u32[]{:S(2)}, u32[]{:S(2)}) async-start(bf16[128,3,2,4,128]{4,3,2,1,0:T(4,128)(2,1)} %constant_dynamic-update-slice_fusion.10), calls=%async_computation.2 | async-start | bytes 1572864 | tf_op jit(solution)/shard_map/all_to_all | solution.py:140
  425.7 4.7 %copy-start.1 = (f32[3,4,32,512]{3,2,1,0:T(8,128)S(1)}, f32[3,4,32,512]{3,2,1,0:T(8,128)}, u32[]{:S(2)}) copy-start(f32[3,4,32,512]{3,2,1,0:T(8,128)} %param.8) | copy-start | bytes 2359300
